TPU v7x, 32 devices: a whole 2x2x4 slice. The times are simulated.
32 devices in a mesh: dp: 2 (over x), row: 4 (over y, core), col: 4 (over z).
Axes of the slice: x: 2, y: 2, z: 4, core: 2. Of those that a mesh axis runs over, the one named last changes fastest.
Arguments:
- tokens: bfloat16 [5120, 2048], P(('dp', 'col'), 'row'), may hold values from -6 to 6
- cotangent: bfloat16 [5120, 2048], P(('dp', 'col'), 'row'), may hold values from -6 to 6
- seg_ids: int32 [5120], P('dp'), may hold values from 0 to 12, as said below
- positions: int32 [5120], P('dp'), may hold values from 0 to 1279, as said below
- parents: int32 [2, 13], P('dp'), may hold values from 0 to 4, as said below
- tree_sets: int32 [2], P('dp'), may hold values from 0 to 7
- gain_q: float32 [2048], P('col'), may hold values from 0.25 to 1.75
- gain_k: float32 [2048], P('col'), may hold values from 0.25 to 1.75
- gain_attn: float32 [2048], P('row'), may hold values from 0.25 to 1.75
- gain_ffn: float32 [2048], P('row'), may hold values from 0.25 to 1.75
- query_key_value_weight: bfloat16 [2048, 3, 2048], P('row', None, 'col'), may hold values from -0.125 to 0.125
- output_weight: bfloat16 [2048, 2048], P('col', 'row'), may hold values from -0.125 to 0.125
- gate_up_weight: bfloat16 [2048, 2, 8192], P('row', None, 'col'), may hold values from -0.125 to 0.125
- down_weight: bfloat16 [8192, 2048], P('col', 'row'), may hold values from -0.0625 to 0.0625
- query_key_value_adapter_first: float32 [3, 8, 16, 2048], P(None, None, None, 'row'), may hold values from -0.125 to 0.125
- query_key_value_adapter_second: float32 [3, 8, 16, 2048], P(None, None, None, 'col'), may hold values from -0.5 to 0.5
- output_adapter_first: float32 [8, 16, 2048], P(None, None, 'col'), may hold values from -0.125 to 0.125
- output_adapter_second: float32 [8, 16, 2048], P(None, None, 'row'), may hold values from -0.5 to 0.5
- gate_up_adapter_first: float32 [2, 8, 16, 2048], P(None, None, None, 'row'), may hold values from -0.125 to 0.125
- gate_up_adapter_second: float32 [2, 8, 16, 8192], P(None, None, None, 'col'), may hold values from -0.5 to 0.5
- down_adapter_first: float32 [8, 16, 8192], P(None, None, 'col'), may hold values from -0.0625 to 0.0625
- down_adapter_second: float32 [8, 16, 2048], P(None, None, 'row'), may hold values from -0.5 to 0.5
Outputs:
- layer_out: bfloat16 [5120, 2048], P(('dp', 'col'), 'row')
- input_grad: float32 [5120, 2048], P(('dp', 'col'), 'row')
- grad_a_qkv: float32 [3, 8, 16, 2048], P(None, 'dp', 'col', 'row')
- grad_b_qkv: float32 [3, 8, 16, 2048], P(None, 'dp', 'row', 'col')
- grad_a_out: float32 [8, 16, 2048], P('dp', 'row', 'col')
- grad_b_out: float32 [8, 16, 2048], P('dp', 'col', 'row')
- grad_a_gu: float32 [2, 8, 16, 2048], P(None, 'dp', 'col', 'row')
- grad_b_gu: float32 [2, 8, 16, 8192], P(None, 'dp', 'row', 'col')
- grad_a_down: float32 [8, 16, 8192], P('dp', 'row', 'col')
- grad_b_down: float32 [8, 16, 2048], P('dp', 'col', 'row')
Inputs may be any that keep to these rules, and one draw needn't show every extreme that they name: `seg_ids`: in each tree the first 1024 tokens are segment 0, the trunk; the other 12 segments of 128 tokens each follow in any order: branches are 1 to 4, leaves the higher numbers. The trunk's tokens have positions 0 to 1023 in order, a branch's 1024 onward, a leaf's 1024 + 128 onward. `parents`: the trunk and the branches have parent 0; each leaf has a branch as parent, and each branch has 2 leaves.
All inputs are finite; a program needn't handle non-finite values.
Results may differ from a plain program's by a relative error of at most 0.025.
Values may be sent and summed in bfloat16 or wider, within the bound.
A program may use at most 320 MiB of HBM per device.

v0:
```python
import jax
import jax.numpy as jnp
from jax import lax
from jax.sharding import PartitionSpec as P

D = 2048
HEAD = 128
RANK = 16
epsilon = 1e-06
rope_base = 500000.0
masked_out = -1e30
low = jnp.bfloat16
wide = jnp.float32
last_last = (((1,), (1,)), ((), ()))
first_first = (((0,), (0,)), ((), ()))


def dot(left, right):
    return jnp.dot(left, right, preferred_element_type=wide)


def dot_t(left, right):
    return lax.dot_general(left, right, last_last, preferred_element_type=wide)


def t_dot(left, right):
    return lax.dot_general(left, right, first_first, preferred_element_type=wide)


def angles(positions):
    half_width = HEAD // 2
    frequency = rope_base ** (-(jnp.arange(half_width, dtype=wide) * 2.0) / HEAD)
    angle_table = positions.astype(wide)[:, None] * frequency[None, :]
    return (jnp.cos(angle_table)[:, None, :], jnp.sin(angle_table)[:, None, :])


def rotate(values, cosine, sine):
    half_width = values.shape[-1] // 2
    first_half = values[..., :half_width]
    second_half = values[..., half_width:]
    return jnp.concatenate(
        [first_half * cosine - second_half * sine, second_half * cosine + first_half * sine],
        axis=-1,
    )


def norm_factor(square_sum):
    return lax.rsqrt(square_sum / D + epsilon)


def norm_back(scaled, flat, factor, cross_sum):
    return factor[:, None] * (scaled - flat * (cross_sum / D)[:, None])


def tree_mask(seg_ids, positions, parents):
    parent_row = parents[0]
    labels = jnp.arange(parent_row.shape[0], dtype=jnp.int32)
    parent_tok = jnp.sum(
        jnp.where(seg_ids[:, None] == labels[None, :], parent_row[None, :], 0), axis=1
    )
    grand_tok = jnp.sum(
        jnp.where(parent_tok[:, None] == labels[None, :], parent_row[None, :], 0), axis=1
    )
    on_path = (
        (seg_ids[None, :] == seg_ids[:, None])
        | (seg_ids[None, :] == parent_tok[:, None])
        | (seg_ids[None, :] == grand_tok[:, None])
    )
    return on_path & (positions[None, :] <= positions[:, None])


def per_device(
    tokens,
    cotangent,
    seg_ids,
    positions,
    parents,
    tree_sets,
    gain_q,
    gain_k,
    gain_attn,
    gain_ffn,
    query_key_value_weight,
    output_weight,
    gate_up_weight,
    down_weight,
    query_key_value_adapter_first,
    query_key_value_adapter_second,
    output_adapter_first,
    output_adapter_second,
    gate_up_adapter_first,
    gate_up_adapter_second,
    down_adapter_first,
    down_adapter_second,
):
    dp_count = lax.axis_size("dp")
    row_count = lax.axis_size("row")
    col_count = lax.axis_size("col")
    row_at = lax.axis_index("row")
    tree_tokens = seg_ids.shape[0]
    assert tree_sets.shape[0] == 1
    set_count = output_adapter_first.shape[0]
    own = tokens.shape[0] // row_count
    group = own * col_count
    width_row = tokens.shape[1]
    width_col = gain_q.shape[0]
    hidden_col = down_weight.shape[0]
    heads_col = width_col // HEAD
    score_scale = HEAD ** (-0.5)
    tree_set = tree_sets[0]

    def pick(table, axis):
        return lax.dynamic_index_in_dim(table, tree_set, axis, keepdims=False)

    narrow = jnp.concatenate(
        [
            pick(query_key_value_adapter_first, 1),
            pick(gate_up_adapter_first, 1),
            pick(output_adapter_second, 0)[None],
            pick(down_adapter_second, 0)[None],
        ],
        axis=0,
    ).astype(low)
    narrow_all = lax.all_gather(narrow, "row", axis=2, tiled=True)
    a_qkv = narrow_all[:3].reshape(3 * RANK, D)
    a_gu = narrow_all[3:5].reshape(2 * RANK, D)
    b_out = narrow_all[5]
    b_down = narrow_all[6]
    b_qkv = pick(query_key_value_adapter_second, 1).astype(low)
    b_gu = pick(gate_up_adapter_second, 1).astype(low)
    a_out = pick(output_adapter_first, 0).astype(low)
    a_down = pick(down_adapter_first, 0).astype(low)
    gains = lax.all_gather(jnp.stack([gain_attn, gain_ffn]), "row", axis=1, tiled=True)
    w_qkv = lax.all_gather(query_key_value_weight, "row", axis=0, tiled=True).reshape(
        D, 3 * width_col
    )
    w_out = lax.all_gather(output_weight, "row", axis=1, tiled=True)
    w_gu = lax.all_gather(gate_up_weight, "row", axis=0, tiled=True).reshape(D, 2 * hidden_col)
    w_down = lax.all_gather(down_weight, "row", axis=1, tiled=True)

    def to_tokens(values):
        return lax.all_to_all(values, "row", split_axis=0, concat_axis=1, tiled=True)

    def to_width(values):
        return lax.all_to_all(values, "row", split_axis=1, concat_axis=0, tiled=True)

    def gather_col(values):
        return lax.all_gather(values, "col", axis=0, tiled=True)

    def scatter_col(values):
        return lax.psum_scatter(values.astype(low), "col", scatter_dimension=0, tiled=True).astype(
            wide
        )

    def to_heads(values, parts):
        by_head = (
            values.reshape(group, parts, heads_col, HEAD)
            .transpose(2, 0, 1, 3)
            .reshape(heads_col, group, parts * HEAD)
        )
        moved = lax.all_to_all(by_head, "row", split_axis=0, concat_axis=0, tiled=True)
        return (
            moved.reshape(row_count, col_count, own, parts * HEAD)
            .transpose(1, 0, 2, 3)
            .reshape(tree_tokens, parts * HEAD)
        )

    def from_heads(values, parts):
        by_row = (
            values.reshape(col_count, row_count, own, parts * HEAD)
            .transpose(1, 0, 2, 3)
            .reshape(row_count, group, parts * HEAD)
        )
        moved = lax.all_to_all(by_row, "row", split_axis=0, concat_axis=0, tiled=True)
        return (
            moved.reshape(heads_col, group, parts, HEAD)
            .transpose(1, 2, 0, 3)
            .reshape(group, parts * width_col)
        )

    x_own = to_tokens(tokens)
    x = gather_col(x_own)
    red_qkv = dot_t(x, a_qkv).astype(low)
    raw = dot(x, w_qkv)
    extra = jnp.concatenate(
        [dot(red_qkv[:, RANK * j : RANK * (j + 1)], b_qkv[j]) for j in range(3)], axis=1
    )
    raw = raw + extra
    q_raw = raw[:, :width_col]
    k_raw = raw[:, width_col : 2 * width_col]
    v_raw = raw[:, 2 * width_col :]
    square_qk = lax.psum(
        jnp.stack([jnp.sum(q_raw * q_raw, axis=1), jnp.sum(k_raw * k_raw, axis=1)]), "col"
    )
    q_factor = norm_factor(square_qk[0])
    k_factor = norm_factor(square_qk[1])
    q_flat = q_raw * q_factor[:, None]
    k_flat = k_raw * k_factor[:, None]
    pos_own = lax.dynamic_index_in_dim(
        positions.reshape(col_count, row_count, own), row_at, 1, keepdims=False
    ).reshape(group)
    cos_own, sin_own = angles(pos_own)

    def turn(values, sine):
        return rotate(values.reshape(group, heads_col, HEAD), cos_own, sine).reshape(
            group, width_col
        )

    q_low = turn(q_flat * gain_q, sin_own).astype(low)
    k_low = turn(k_flat * gain_k, sin_own).astype(low)
    qkv_head = to_heads(jnp.concatenate([q_low, k_low, v_raw.astype(low)], axis=1), 3)
    q_head = qkv_head[:, :HEAD]
    k_head = qkv_head[:, HEAD : 2 * HEAD]
    v_head = qkv_head[:, 2 * HEAD :]
    visible = tree_mask(seg_ids, positions, parents)
    scores = jnp.where(visible, dot_t(q_head, k_head) * score_scale, masked_out)
    highest = jnp.max(scores, axis=1, keepdims=True)
    raised = jnp.exp(scores - highest)
    probs = raised / jnp.sum(raised, axis=1, keepdims=True)
    probs_low = probs.astype(low)
    attn_head = dot(probs_low, v_head).astype(low)
    attn = from_heads(attn_head, 1)
    red_out = dot_t(attn, a_out).astype(low)
    a_raw = scatter_col(dot(attn, w_out) + dot(red_out, b_out))
    a_factor = norm_factor(jnp.sum(a_raw * a_raw, axis=1))
    a_flat = a_raw * a_factor[:, None]
    h_own = x_own.astype(wide) + a_flat * gains[0]
    h = gather_col(h_own.astype(low))
    red_gu = dot_t(h, a_gu).astype(low)
    gate = dot(h, w_gu[:, :hidden_col]) + dot(red_gu[:, :RANK], b_gu[0])
    up = dot(h, w_gu[:, hidden_col:]) + dot(red_gu[:, RANK:], b_gu[1])
    sigma = jax.nn.sigmoid(gate)
    hidden = (gate * sigma * up).astype(low)
    red_down = dot_t(hidden, a_down).astype(low)
    f_raw = scatter_col(dot(hidden, w_down) + dot(red_down, b_down))
    f_factor = norm_factor(jnp.sum(f_raw * f_raw, axis=1))
    f_flat = f_raw * f_factor[:, None]
    out_own = (h_own + f_flat * gains[1]).astype(low)
    layer_out = to_width(out_own)
    g_own = to_tokens(cotangent).astype(wide)
    scaled_f = g_own * gains[1]
    d_f_own = norm_back(scaled_f, f_flat, f_factor, jnp.sum(scaled_f * f_flat, axis=1)).astype(low)
    d_f = gather_col(d_f_own)
    back_down = dot_t(d_f, b_down).astype(low)
    d_hidden = dot_t(d_f, w_down) + dot(back_down, a_down)
    d_gate = (d_hidden * up * sigma * (1.0 + gate * (1.0 - sigma))).astype(low)
    d_up = (d_hidden * (gate * sigma)).astype(low)
    back_gate = dot_t(d_gate, b_gu[0]).astype(low)
    back_up = dot_t(d_up, b_gu[1]).astype(low)
    back_gu = jnp.concatenate([back_gate, back_up], axis=1)
    d_h = g_own + scatter_col(
        dot_t(d_gate, w_gu[:, :hidden_col]) + dot_t(d_up, w_gu[:, hidden_col:]) + dot(back_gu, a_gu)
    )
    scaled_a = d_h * gains[0]
    d_a_own = norm_back(scaled_a, a_flat, a_factor, jnp.sum(scaled_a * a_flat, axis=1)).astype(low)
    d_a = gather_col(d_a_own)
    back_out = dot_t(d_a, b_out).astype(low)
    d_attn = (dot_t(d_a, w_out) + dot(back_out, a_out)).astype(low)
    d_attn_head = to_heads(d_attn, 1)
    d_probs = dot_t(d_attn_head, v_head)
    inner = jnp.sum(probs * d_probs, axis=1, keepdims=True)
    d_scores = (probs * (d_probs - inner)).astype(low)
    dq_head = (dot(d_scores, k_head) * score_scale).astype(low)
    dk_head = (t_dot(d_scores, q_head) * score_scale).astype(low)
    dv_head = t_dot(probs_low, d_attn_head).astype(low)
    d_qkv = from_heads(jnp.concatenate([dq_head, dk_head, dv_head], axis=1), 3)
    dq_n = turn(d_qkv[:, :width_col].astype(wide), -sin_own) * gain_q
    dk_n = turn(d_qkv[:, width_col : 2 * width_col].astype(wide), -sin_own) * gain_k
    cross_qk = lax.psum(
        jnp.stack([jnp.sum(dq_n * q_flat, axis=1), jnp.sum(dk_n * k_flat, axis=1)]), "col"
    )
    d_q = norm_back(dq_n, q_flat, q_factor, cross_qk[0]).astype(low)
    d_k = norm_back(dk_n, k_flat, k_factor, cross_qk[1]).astype(low)
    d_v = d_qkv[:, 2 * width_col :]
    d_raw = jnp.concatenate([d_q, d_k, d_v], axis=1)
    back_qkv = jnp.concatenate(
        [dot_t(d, b) for d, b in zip((d_q, d_k, d_v), (b_qkv[0], b_qkv[1], b_qkv[2]))], axis=1
    ).astype(low)
    in_own = d_h + scatter_col(dot_t(d_raw, w_qkv) + dot(back_qkv, a_qkv))
    input_grad = to_width(in_own.astype(low)).astype(wide)
    full_width = jnp.concatenate(
        [t_dot(back_qkv, x), t_dot(back_gu, h), t_dot(red_out, d_a), t_dot(red_down, d_f)], axis=0
    ).astype(low)
    full_width = lax.psum_scatter(full_width, "row", scatter_dimension=1, tiled=True)
    full_width = full_width.reshape(7, col_count, RANK // col_count, width_row).transpose(
        1, 0, 2, 3
    )
    full_width = lax.psum_scatter(full_width, "col", scatter_dimension=0, tiled=False)
    col_width = jnp.concatenate(
        [t_dot(red_qkv[:, RANK * j : RANK * (j + 1)], d) for j, d in enumerate((d_q, d_k, d_v))]
        + [
            t_dot(back_out, attn),
            t_dot(red_gu[:, :RANK], d_gate),
            t_dot(red_gu[:, RANK:], d_up),
            t_dot(back_down, hidden),
        ],
        axis=1,
    ).astype(low)
    col_width = lax.psum_scatter(col_width, "row", scatter_dimension=0, tiled=True)
    onehot = (tree_set == jnp.arange(set_count, dtype=jnp.int32)).astype(wide)
    owner = jnp.concatenate([full_width.reshape(-1), col_width.reshape(-1)])
    owner_all = lax.all_gather(owner, "dp", axis=0, tiled=False).astype(wide)
    onehot_all = lax.all_gather(onehot, "dp", axis=0, tiled=False)
    sets_own = set_count // dp_count
    onehot_own = lax.dynamic_slice_in_dim(onehot_all, lax.axis_index("dp") * sets_own, sets_own, 1)
    per_set = jnp.sum(onehot_own[:, :, None] * owner_all[:, None, :], axis=0)
    split_at = full_width.size
    full_sets = per_set[:, :split_at].reshape(sets_own, 7, RANK // col_count, width_row)
    col_sets = per_set[:, split_at:].reshape(sets_own, RANK // row_count, -1)
    grad_a_qkv = full_sets[:, :3].transpose(1, 0, 2, 3)
    grad_a_gu = full_sets[:, 3:5].transpose(1, 0, 2, 3)
    grad_b_out = full_sets[:, 5]
    grad_b_down = full_sets[:, 6]
    grad_b_qkv = jnp.stack([col_sets[..., width_col * j : width_col * (j + 1)] for j in range(3)])
    grad_a_out = col_sets[..., 3 * width_col : 4 * width_col]
    gu_at = 4 * width_col
    grad_b_gu = jnp.stack(
        [col_sets[..., gu_at + hidden_col * j : gu_at + hidden_col * (j + 1)] for j in range(2)]
    )
    grad_a_down = col_sets[..., gu_at + 2 * hidden_col :]
    return (
        layer_out,
        input_grad,
        grad_a_qkv,
        grad_b_qkv,
        grad_a_out,
        grad_b_out,
        grad_a_gu,
        grad_b_gu,
        grad_a_down,
        grad_b_down,
    )


def solution(mesh):
    in_specs = (
        P(("dp", "col"), "row"),
        P(("dp", "col"), "row"),
        P("dp"),
        P("dp"),
        P("dp", None),
        P("dp"),
        P("col"),
        P("col"),
        P("row"),
        P("row"),
        P("row", None, "col"),
        P("col", "row"),
        P("row", None, "col"),
        P("col", "row"),
        P(None, None, None, "row"),
        P(None, None, None, "col"),
        P(None, None, "col"),
        P(None, None, "row"),
        P(None, None, None, "row"),
        P(None, None, None, "col"),
        P(None, None, "col"),
        P(None, None, "row"),
    )
    out_specs = (
        P(("dp", "col"), "row"),
        P(("dp", "col"), "row"),
        P(None, "dp", "col", "row"),
        P(None, "dp", "row", "col"),
        P("dp", "row", "col"),
        P("dp", "col", "row"),
        P(None, "dp", "col", "row"),
        P(None, "dp", "row", "col"),
        P("dp", "row", "col"),
        P("dp", "col", "row"),
    )
    return jax.shard_map(
        per_device, mesh=mesh, in_specs=in_specs, out_specs=out_specs, check_vma=False
    )
```

profile of v0, /device:TPU:0, one launch (start us, length us, event | category | flops | bytes accessed | tf_op | source)
XLA Modules:
  0.0 1157.8 jit_solution(14469267757178420043)
XLA Ops:
  7.2 14.6 %all_to_all.84 = bf16[4,160,512]{2,1,0:T(8,128)(2,1)S(1)} all-to-all(bf16[4,160,512]{2,1,0:T(8,128)(2,1)} %bitcast.270), channel_id=1, replica_groups=mesh['dp'=2,'row'=4,'col'=4] {'row'}, dimensions={0} | all-to-all | bytes 1310720 | tf_op jit(solution)/shard_map/all_to_all | solution.py:142
  39.2 39.6 %all-gather.11.cloned.1.call-done = bf16[640,2048]{1,0:T(8,128)(2,1)} async-done(((bf16[160,2048]{1,0:T(8,128)(2,1)}), bf16[640,2048]{1,0:T(8,128)(2,1)}) %all-gather.11.cloned.1.call-update) | async-done | bytes 2621456 | tf_op jit(solution)/shard_map/all_gather | solution.py:148
  84.6 40.9 %all-gather.13.cloned.1.call-done = bf16[2048,3,512]{0,2,1:T(8,128)(2,1)} async-done(((bf16[512,3,512]{0,2,1:T(8,128)(2,1)}), bf16[2048,3,512]{0,2,1:T(8,128)(2,1)}) %all-gather.13.cloned.1.call-update) | async-done | bytes 6291472 | tf_op jit(solution)/shard_map/all_gather | solution.py:134
  137.0 12.3 %psum.14 = f32[2,640]{1,0:T(2,128)S(1)} all-reduce(f32[2,640]{1,0:T(2,128)S(1)} %pad_maximum_fusion.17), channel_id=1, replica_groups=mesh['dp'=2,'row'=4,'col'=4] {'col'}, use_global_device_ids=true, to_apply=%region_4.5 | all-reduce | flops 1280 | bytes 10240 | tf_op jit(solution)/shard_map/psum | solution.py:192
  179.6 34.4 %all-to-all-done.1 = bf16[4,640,384]{1,2,0:T(8,128)(2,1)} async-done(((bf16[4,640,384]{1,2,0:T(8,128)(2,1)}), bf16[4,640,384]{1,2,0:T(8,128)(2,1)}, u32[]{:S(2)}, u32[]{:S(2)}) %all-to-all-start.1) | async-done | bytes 1966112 | tf_op jit(solution)/shard_map/all_to_all | solution.py:161
  228.3 8.6 copy-done.2
  240.8 10.9 fusion.15
  251.8 12.7 %all_to_all.85 = bf16[4,640,128]{2,1,0:T(8,128)(2,1)S(1)} all-to-all(bf16[4,640,128]{2,1,0:T(8,128)(2,1)S(1)} %bitcast.254), channel_id=1, replica_groups=mesh['dp'=2,'row'=4,'col'=4] {'row'}, dimensions={0} | all-to-all | bytes 1310720 | tf_op jit(solution)/shard_map/all_to_all | solution.py:174
  278.0 43.6 %reduce-scatter.7.cloned.1.call-done = bf16[160,2048]{1,0:T(8,128)(2,1)} async-done(((bf16[640,2048]{1,0:T(8,128)(2,1)}), bf16[160,2048]{1,0:T(8,128)(2,1)}) %reduce-scatter.7.cloned.1.call-update) | async-done | bytes 655376 | tf_op jit(solution)/shard_map/reduce_scatter | solution.py:151
  327.8 52.1 %all-gather.17.cloned.1.call-done = bf16[640,2048]{1,0:T(8,128)(2,1)} async-done(((bf16[160,2048]{1,0:T(8,128)(2,1)}), bf16[640,2048]{1,0:T(8,128)(2,1)}) %all-gather.17.cloned.1.call-update) | async-done | bytes 2621456 | tf_op jit(solution)/shard_map/all_gather | solution.py:148
  382.5 103.5 %all-gather.19.cloned.1.call-done = bf16[2048,2,2048]{2,1,0:T(2,128)(2,1)} async-done(((bf16[512,2,2048]{2,1,0:T(2,128)(2,1)}), bf16[2048,2,2048]{2,1,0:T(2,128)(2,1)}) %all-gather.19.cloned.1.call-update) | async-done | bytes 16777232 | tf_op jit(solution)/shard_map/all_gather | solution.py:138
  486.0 13.0 %copy.133 = bf16[256,8,2,2048]{3,1,2,0:T(8,128)(2,1)S(1)} copy(bf16[256,8,2,2048]{3,2,1,0:T(2,128)(2,1)} %bitcast.231) | data formatting | bytes 33554432
  525.4 20.5 %all-gather.21.cloned.1.call-done = bf16[2048,2048]{1,0:T(8,128)(2,1)} async-done(((bf16[2048,512]{1,0:T(8,128)(2,1)}), bf16[2048,2048]{1,0:T(8,128)(2,1)}) %all-gather.21.cloned.1.call-update) | async-done | bytes 8388624 | tf_op jit(solution)/shard_map/all_gather | solution.py:139
  545.9 8.8 fusion.116
  559.0 12.6 %all_to_all.86 = bf16[4,160,512]{2,1,0:T(8,128)(2,1)S(1)} all-to-all(bf16[4,160,512]{2,1,0:T(8,128)(2,1)S(1)} %bitcast.271), channel_id=1, replica_groups=mesh['dp'=2,'row'=4,'col'=4] {'row'}, dimensions={0} | all-to-all | bytes 1310720 | tf_op jit(solution)/shard_map/all_to_all | solution.py:142
  571.9 38.2 %reduce-scatter.9.cloned.1.call-done = bf16[160,2048]{1,0:T(8,128)(2,1)} async-done(((bf16[640,2048]{1,0:T(8,128)(2,1)}), bf16[160,2048]{1,0:T(8,128)(2,1)}) %reduce-scatter.9.cloned.1.call-update) | async-done | bytes 655376 | tf_op jit(solution)/shard_map/reduce_scatter | solution.py:151
  614.8 54.1 %all-gather.23.cloned.1.call-done = bf16[640,2048]{1,0:T(8,128)(2,1)} async-done(((bf16[160,2048]{1,0:T(8,128)(2,1)}), bf16[640,2048]{1,0:T(8,128)(2,1)}) %all-gather.23.cloned.1.call-update) | async-done | bytes 2621456 | tf_op jit(solution)/shard_map/all_gather | solution.py:148
  668.9 11.2 fusion.117
  681.9 9.8 multiply_convert_fusion.1
  716.6 51.0 %reduce-scatter.11.cloned.1.call-done = bf16[160,2048]{1,0:T(8,128)(2,1)} async-done(((bf16[640,2048]{1,0:T(8,128)(2,1)}), bf16[160,2048]{1,0:T(8,128)(2,1)}) %reduce-scatter.11.cloned.1.call-update) | async-done | bytes 655376 | tf_op jit(solution)/shard_map/reduce_scatter | solution.py:151
  772.2 54.6 %all-gather.25.cloned.1.call-done = bf16[640,2048]{1,0:T(8,128)(2,1)} async-done(((bf16[160,2048]{1,0:T(8,128)(2,1)}), bf16[640,2048]{1,0:T(8,128)(2,1)}) %all-gather.25.cloned.1.call-update) | async-done | bytes 2621456 | tf_op jit(solution)/shard_map/all_gather | solution.py:148
  834.3 12.8 %all_to_all.87 = bf16[4,640,128]{2,1,0:T(8,128)(2,1)S(1)} all-to-all(bf16[4,640,128]{2,1,0:T(8,128)(2,1)S(1)} %bitcast.256), channel_id=1, replica_groups=mesh['dp'=2,'row'=4,'col'=4] {'row'}, dimensions={0} | all-to-all | bytes 1310720 | tf_op jit(solution)/shard_map/all_to_all | solution.py:161
  847.2 11.3 fusion.20
  858.5 20.5 %multiply_reduce_fusion = (f32[2560]{0:T(1024)S(1)}, f32[2560,2560]{0,1:T(8,128)}) fusion(f32[2560]{0:T(1024)S(1)} %copy-done.64, f32[2560,2560]{0,1:T(8,128)} %copy-done.2, f32[2560]{0:T(1024)S(1)} %copy-done.62, bf16[2560,128]{1,0:T(8,128)(2,1)S(1)} %bitcast.273, bf16[2560,384]{1,0:T(8,128)(2,1)S(1)} %bitcast.249), kind=kOutput, calls=%fused_computation.1 | convolution fusion | flops 1703933440 | bytes 53774336 | tf_op jit(solution)/shard_map/dot_general | solution.py:23
  878.9 22.4 %multiply_convert_fusion = bf16[2560,2560]{0,1:T(8,128)(2,1)} fusion(f32[2560,2560]{0,1:T(8,128)} %get-tuple-element.100, f32[2560]{0:T(1024)S(1)} %get-tuple-element.99, f32[2560]{0:T(1024)S(1)} %copy-done.64, f32[2560,2560]{0,1:T(8,128)} %copy-done.2, f32[2560]{0:T(1024)S(1)} %copy-done.62), kind=kLoop, calls=%fused_computation | loop fusion | flops 32768000 | bytes 65566720 | tf_op jit(solution)/shard_map/convert_element_type | solution.py:262
  901.3 9.1 fusion.18
  933.0 17.8 %all-to-all-done.6 = bf16[4,640,384]{2,1,0:T(8,128)(2,1)S(1)} async-done(((bf16[4,640,384]{2,1,0:T(8,128)(2,1)}), bf16[4,640,384]{2,1,0:T(8,128)(2,1)S(1)}, u32[]{:S(2)}, u32[]{:S(2)}) %all-to-all-start.6) | async-done | bytes 1966112 | tf_op jit(solution)/shard_map/all_to_all | solution.py:174
  971.6 9.6 psum.15
  993.5 8.8 fusion.26
  1028.9 12.6 %all-reduce.7.cloned.1.call-done = bf16[16,8192]{1,0:T(8,128)(2,1)} async-done(((bf16[16,8192]{1,0:T(8,128)(2,1)}), bf16[16,8192]{1,0:T(8,128)(2,1)}) %all-reduce.7.cloned.1.call-update) | async-done | bytes 262160
  1042.4 36.0 %all-reduce.5.cloned.1.call-done = bf16[4,7,4,512]{3,2,0,1:T(4,128)(2,1)} async-done(((bf16[4,7,4,512]{3,2,0,1:T(4,128)(2,1)}), bf16[4,7,4,512]{3,2,0,1:T(4,128)(2,1)}) %all-reduce.5.cloned.1.call-update) | async-done | bytes 114704
  1091.2 41.5 %reduce-scatter.13.cloned.1.call-done = bf16[160,2048]{1,0:T(8,128)(2,1)} async-done(((bf16[640,2048]{1,0:T(8,128)(2,1)}), bf16[160,2048]{1,0:T(8,128)(2,1)}) %reduce-scatter.13.cloned.1.call-update) | async-done | bytes 655376 | tf_op jit(solution)/shard_map/reduce_scatter | solution.py:151
  (348 shorter events, 291.6 us)
Async XLA Ops:
  7.2 320.6 %copy-start = (f32[2,8,16,2048]{3,2,1,0:T(8,128)S(1)}, f32[2,8,16,2048]{3,2,1,0:T(8,128)}, u32[]{:S(2)}) copy-start(f32[2,8,16,2048]{3,2,1,0:T(8,128)} %param.41) | copy-start | bytes 6291460
  7.2 71.5 %all-gather.11.cloned.1.call-start = ((), (), s32[]{:S(2)}) async-start(), calls=%async_computation.13 | async-start | bytes 3276800 | tf_op jit(solution)/shard_map/all_gather | solution.py:148
  22.8 102.7 %all-gather.13.cloned.1.call-start = ((), (), s32[]{:S(2)}) async-start(), calls=%async_computation.14 | async-start | bytes 7864320 | tf_op jit(solution)/shard_map/all_gather | solution.py:134
  36.0 46.7 %copy-start.34 = (bf16[3,16,2048]{2,1,0:T(8,128)(2,1)}, bf16[3,16,2048]{2,1,0:T(8,128)(2,1)S(1)}, u32[]{:S(2)}) copy-start(bf16[3,16,2048]{2,1,0:T(8,128)(2,1)S(1)} %slice.228) | copy-start | bytes 589828
  37.0 47.2 %copy-start.43 = (bf16[3,1,16,512]{3,2,1,0:T(8,128)(2,1)}, bf16[3,1,16,512]{3,2,1,0:T(8,128)(2,1)S(1)}, u32[]{:S(2)}) copy-start(bf16[3,1,16,512]{3,2,1,0:T(8,128)(2,1)S(1)} %dynamic-slice_convert_fusion.2) | copy-start | bytes 147460
  173.8 40.1 %all-to-all-start.1 = ((bf16[4,640,384]{1,2,0:T(8,128)(2,1)}), bf16[4,640,384]{1,2,0:T(8,128)(2,1)}, u32[]{:S(2)}, u32[]{:S(2)}) async-start(bf16[4,640,384]{1,2,0:T(8,128)(2,1)} %bitcast.242), calls=%async_computation.1 | async-start | bytes 3932160 | tf_op jit(solution)/shard_map/all_to_all | solution.py:161
  178.4 87.4 %all-gather.15.cloned.1.call-start = ((), (), s32[]{:S(2)}) async-start(), calls=%async_computation.15 | async-start | bytes 2621440 | tf_op jit(solution)/shard_map/all_gather | solution.py:137
  179.1 142.5 %reduce-scatter.7.cloned.1.call-start = ((), (), s32[]{:S(2)}) async-start(), calls=%async_computation.16 | async-start | bytes 3276800 | tf_op jit(solution)/shard_map/reduce_scatter | solution.py:151
  219.8 21.0 %copy-start.28 = (bf16[4,4,160,384]{3,2,1,0:T(8,128)(2,1)}, bf16[4,4,160,384]{3,2,1,0:T(8,128)(2,1)S(1)}, u32[]{:S(2)}) copy-start(bf16[4,4,160,384]{3,2,1,0:T(8,128)(2,1)S(1)} %copy.108) | copy-start | bytes 5898244
  272.1 50.8 %copy-start.20 = (bf16[4,20,8,512]{3,2,0,1:T(8,128)(2,1)S(1)}, bf16[4,20,8,512]{3,2,0,1:T(8,128)(2,1)}, u32[]{:S(2)}) copy-start(bf16[4,20,8,512]{3,2,0,1:T(8,128)(2,1)} %copy.129) | copy-start | bytes 1966084
  272.1 107.7 %all-gather.17.cloned.1.call-start = ((), (), s32[]{:S(2)}) async-start(), calls=%async_computation.17 | async-start | bytes 3276800 | tf_op jit(solution)/shard_map/all_gather | solution.py:148
  325.2 160.8 %all-gather.19.cloned.1.call-start = ((), (), s32[]{:S(2)}) async-start(), calls=%async_computation.18 | async-start | bytes 20971520 | tf_op jit(solution)/shard_map/all_gather | solution.py:138
  325.8 220.1 %all-gather.21.cloned.1.call-start = ((), (), s32[]{:S(2)}) async-start(), calls=%async_computation.19 | async-start | bytes 10485760 | tf_op jit(solution)/shard_map/all_gather | solution.py:139
  326.6 283.6 %reduce-scatter.9.cloned.1.call-start = ((), (), s32[]{:S(2)}) async-start(), calls=%async_computation.20 | async-start | bytes 3276800 | tf_op jit(solution)/shard_map/reduce_scatter | solution.py:151
  382.5 134.7 %copy-start.48 = (bf16[640,32]{0,1:T(8,128)(2,1)}, bf16[640,32]{0,1:T(8,128)(2,1)S(1)}, u32[]{:S(2)}) copy-start(bf16[640,32]{0,1:T(8,128)(2,1)S(1)} %convolution_convert_fusion.8) | copy-start | bytes 122884
  525.4 29.3 %copy-start.50 = (bf16[640,16]{0,1:T(8,128)(2,1)}, bf16[640,16]{0,1:T(8,128)(2,1)S(1)}, u32[]{:S(2)}) copy-start(bf16[640,16]{0,1:T(8,128)(2,1)S(1)} %convolution_convert_fusion.17) | copy-start | bytes 61444
  557.9 111.0 %all-gather.23.cloned.1.call-start = ((), (), s32[]{:S(2)}) async-start(), calls=%async_computation.21 | async-start | bytes 3276800 | tf_op jit(solution)/shard_map/all_gather | solution.py:148
  571.9 197.2 %copy-start.3 = (f32[4,20,8,512]{3,2,0,1:T(8,128)}, f32[4,20,8,512]{3,2,0,1:T(8,128)S(1)}, u32[]{:S(2)}) copy-start(f32[4,20,8,512]{3,2,0,1:T(8,128)S(1)} %copy.130) | copy-start | bytes 3932164
  614.3 153.3 %reduce-scatter.11.cloned.1.call-start = ((), (), s32[]{:S(2)}) async-start(), calls=%async_computation.22 | async-start | bytes 3276800 | tf_op jit(solution)/shard_map/reduce_scatter | solution.py:151
  716.5 51.1 %copy-start.21 = (bf16[160,2048]{1,0:T(8,128)(2,1)S(1)}, bf16[160,2048]{1,0:T(8,128)(2,1)}, u32[]{:S(2)}) copy-start(bf16[160,2048]{1,0:T(8,128)(2,1)} %reduce-scatter.7.cloned.1.call-done) | copy-start | bytes 1966084
  716.5 110.3 %all-gather.25.cloned.1.call-start = ((), (), s32[]{:S(2)}) async-start(), calls=%async_computation.23 | async-start | bytes 3276800 | tf_op jit(solution)/shard_map/all_gather | solution.py:148
  922.8 28.0 %all-to-all-start.6 = ((bf16[4,640,384]{2,1,0:T(8,128)(2,1)}), bf16[4,640,384]{2,1,0:T(8,128)(2,1)S(1)}, u32[]{:S(2)}, u32[]{:S(2)}) async-start(bf16[4,640,384]{2,1,0:T(8,128)(2,1)} %bitcast.243), calls=%async_computation.9 | async-start | bytes 3932160 | tf_op jit(solution)/shard_map/all_to_all | solution.py:174
  926.6 79.7 %reduce-scatter.15.cloned.1.call-start = ((), (), s32[]{:S(2)}) async-start(), calls=%async_computation.25 | async-start | bytes 573440 | tf_op jit(solution)/shard_map/reduce_scatter | solution.py:284
  987.2 54.2 %all-reduce.7.cloned.1.call-start = ((), (), s32[]{:S(2)}) async-start(), calls=%async_computation.27 | async-start | bytes 524288
  993.5 84.9 %all-reduce.5.cloned.1.call-start = ((), (), s32[]{:S(2)}) async-start(), calls=%async_computation.26 | async-start | bytes 229376
  1007.8 124.9 %reduce-scatter.13.cloned.1.call-start = ((), (), s32[]{:S(2)}) async-start(), calls=%async_computation.24 | async-start | bytes 3276800 | tf_op jit(solution)/shard_map/reduce_scatter | solution.py:151
  1014.8 14.1 %all-to-all-start.3 = ((bf16[160,4,512]{2,0,1:T(8,128)(2,1)}), bf16[160,4,512]{2,0,1:T(8,128)(2,1)S(1)}, u32[]{:S(2)}, u32[]{:S(2)}) async-start(bf16[160,4,512]{2,0,1:T(8,128)(2,1)} %bitcast.215), calls=%async_computation.5 | async-start | bytes 1310720 | tf_op jit(solution)/shard_map/all_to_all | solution.py:145
  1085.3 47.4 %copy-start.4 = (f32[4,20,8,512]{3,2,0,1:T(8,128)S(1)}, f32[4,20,8,512]{3,2,0,1:T(8,128)}, u32[]{:S(2)}) copy-start(f32[4,20,8,512]{3,2,0,1:T(8,128)} %copy-done.3) | copy-start | bytes 3932164
  1085.4 47.4 %copy-start.26 = (bf16[160,2048]{1,0:T(8,128)(2,1)S(1)}, bf16[160,2048]{1,0:T(8,128)(2,1)}, u32[]{:S(2)}) copy-start(bf16[160,2048]{1,0:T(8,128)(2,1)} %reduce-scatter.11.cloned.1.call-done) | copy-start | bytes 1966084
  1086.9 47.2 %copy-start.37 = (f32[4,7,4,512]{3,2,1,0:T(4,128)}, f32[4,7,4,512]{3,2,1,0:T(4,128)S(1)}, u32[]{:S(2)}) copy-start(f32[4,7,4,512]{3,2,1,0:T(4,128)S(1)} %reshape.348) | copy-start | bytes 688132
  1135.0 15.9 %copy-start.1 = (f32[2,8,16,2048]{3,2,1,0:T(8,128)S(1)}, f32[2,8,16,2048]{3,2,1,0:T(8,128)}, u32[]{:S(2)}) copy-start(f32[2,8,16,2048]{3,2,1,0:T(8,128)} %param.41) | copy-start | bytes 6291460
  1135.0 13.8 %all-to-all-start.7 = ((bf16[160,4,512]{2,0,1:T(8,128)(2,1)}), bf16[160,4,512]{2,0,1:T(8,128)(2,1)S(1)}, u32[]{:S(2)}, u32[]{:S(2)}) async-start(bf16[160,4,512]{2,0,1:T(8,128)(2,1)} %bitcast.214), calls=%async_computation.11 | async-start | bytes 1310720 | tf_op jit(solution)/shard_map/all_to_all | solution.py:145
  (67 other events, 376.3 us)
Sparse Core Ops, SparseCore 0:
  22.9 55.7 all-gather.10
  80.3 45.1 all-gather.12
  180.8 32.5 all-gather.14
  272.3 49.3 reduce-scatter.6
  325.3 54.4 all-gather.16
  381.3 104.6 all-gather.18
  487.6 58.2 all-gather.20
  558.1 52.0 reduce-scatter.8
  614.4 54.4 all-gather.22
  716.7 50.8 reduce-scatter.10
  772.3 54.4 all-gather.24
  987.4 18.8 reduce-scatter.14
  1009.1 32.2 all-reduce.6
  1044.3 34.0 all-reduce.4
  1080.6 52.0 reduce-scatter.12
where the time goes:
time: 1170 us; the launch traced here: 1160 us
  waiting for transfers between devices  654 us (56%)
  matrix products  212 us (18%)
  local copies, waits for them, and re-layouts  96.2 us (8%)
  blocking collectives  95.6 us (8%)
  other arithmetic  66.5 us (6%)
  starting transfers between devices  16.8 us (1%)
  between operations  16.8 us (1%)
    all_gather x4, waiting for transfers between devices, gather_col(): return lax.all_gather(values, 'col', axis=0, tiled=True)  200 us
    reduce_scatter x4, waiting for transfers between devices, scatter_col(): lax.psum_scatter(values.astype(low), 'col', scatter_dimension=0, tiled=True)  174 us
    all_gather x1, waiting for transfers between devices, per_device(): lax.all_gather(gate_up_weight, 'row', axis=0, tiled=True)  104 us
    dot_general x18, matrix products, dot(): return jnp.dot(left, right, preferred_element_type=wide)  93.1 us
    dot_general x18, matrix products, dot_t(): return lax.dot_general(left, right, last_last, preferred_element_type=wide)  84.5 us
    unnamed x17, waiting for transfers between devices  50.7 us
    unnamed x173, local copies, waits for them, and re-layouts  41 us
    all_gather x1, waiting for transfers between devices, per_device(): lax.all_gather(query_key_value_weight, 'row', axis=0, tiled=True)  40.9 us
  transfers between devices with their start and end apart: 19, of which 18 were waited for; matrix products, arithmetic and copies ran while one was open for 11% of the time, Pallas kernels for 0%

commit v1 on v0

--- a/solution.py
+++ b/solution.py
@@ -13,6 +13,27 @@
 wide = jnp.float32
 last_last = (((1,), (1,)), ((), ()))
 first_first = (((0,), (0,)), ((), ()))
+
+
+def ring_gather(x, axis, dim):
+    size, position, rows = (lax.axis_size(axis), lax.axis_index(axis), x.shape[dim])
+    ahead = [(i, (i + 1) % size) for i in range(size)]
+    backward = [(i, (i - 1) % size) for i in range(size)]
+    filled = jnp.zeros((*x.shape[:dim], size * rows, *x.shape[dim + 1 :]), x.dtype)
+    filled = lax.dynamic_update_slice_in_dim(filled, x, position * rows, axis=dim)
+    from_left = from_right = x
+    middle = size // 2
+    for step in range(1, middle + 1):
+        from_left = lax.ppermute(from_left, axis, ahead)
+        filled = lax.dynamic_update_slice_in_dim(
+            filled, from_left, (position - step) % size * rows, axis=dim
+        )
+        if step < size - middle:
+            from_right = lax.ppermute(from_right, axis, backward)
+            filled = lax.dynamic_update_slice_in_dim(
+                filled, from_right, (position + step) % size * rows, axis=dim
+            )
+    return filled
 
 
 def dot(left, right):
@@ -145,7 +166,7 @@
         return lax.all_to_all(values, "row", split_axis=1, concat_axis=0, tiled=True)
 
     def gather_col(values):
-        return lax.all_gather(values, "col", axis=0, tiled=True)
+        return ring_gather(values, "col", 0)
 
     def scatter_col(values):
         return lax.psum_scatter(values.astype(low), "col", scatter_dimension=0, tiled=True).astype(

time: 1170 us -> 1030 us (0.88)
  waiting for transfers between devices: 654 us -> 483 us
  starting transfers between devices: 16.8 us -> 71.7 us
  blocking collectives: 95.6 us -> 81.7 us
    all_gather x4 -> x0, waiting for transfers between devices: 200 us -> none  [gather_col(): return lax.all_gather(values, 'col', axis=0, tiled=True)]
    ppermute x0 -> x12, waiting for transfers between devices: none -> 119 us  [the longest x8 105 us: ring_gather(): from_left = lax.ppermute(from_left, axis, ahead)]
    all_gather x1, waiting for transfers between devices: 104 us -> 51.2 us  [per_device(): lax.all_gather(gate_up_weight, 'row', axis=0, tiled=True)]
    ppermute x0 -> x12, starting transfers between devices: none -> 51 us  [the longest x8 39.3 us: ring_gather(): from_left = lax.ppermute(from_left, axis, ahead)]
    all_gather x1, waiting for transfers between devices: 40.9 us -> 0.01 us  [per_device(): lax.all_gather(query_key_value_weight, 'row', axis=0, tiled=True)]
    all_to_all x2 -> x1, blocking collectives: 27.3 us -> 12.6 us  [to_tokens(): lax.all_to_all(values, 'row', split_axis=0, concat_axis=1, tiled=True)]
    unnamed x17 -> x13, waiting for transfers between devices: 50.7 us -> 50.3 us
    unnamed x173 -> x189, local copies, waits for them, and re-layouts: 41 us -> 40.6 us
  transfers between devices with their start and end apart: 19 -> 28, of which waited for: 18 -> 26; matrix products, arithmetic and copies ran while one was open for 11% -> 14% of each run, Pallas kernels for 0% -> 0%
where the time goes in v1:
time: 1030 us; the launch traced here: 1020 us
  waiting for transfers between devices  483 us (47%)
  matrix products  206 us (20%)
  local copies, waits for them, and re-layouts  99.7 us (10%)
  blocking collectives  81.7 us (8%)
  starting transfers between devices  71.7 us (7%)
  other arithmetic  62.6 us (6%)
  between operations  17 us (2%)
    reduce_scatter x4, waiting for transfers between devices, scatter_col(): lax.psum_scatter(values.astype(low), 'col', scatter_dimension=0, tiled=True)  172 us
    ppermute x8, waiting for transfers between devices, ring_gather(): from_left = lax.ppermute(from_left, axis, ahead)  105 us
    dot_general x18, matrix products, dot(): return jnp.dot(left, right, preferred_element_type=wide)  87 us
    dot_general x18, matrix products, dot_t(): return lax.dot_general(left, right, last_last, preferred_element_type=wide)  83.4 us
    all_gather x1, waiting for transfers between devices, per_device(): lax.all_gather(gate_up_weight, 'row', axis=0, tiled=True)  51.2 us
    unnamed x13, waiting for transfers between devices  50.3 us
    unnamed x189, local copies, waits for them, and re-layouts  40.6 us
    ppermute x8, starting transfers between devices, ring_gather(): from_left = lax.ppermute(from_left, axis, ahead)  39.3 us
  transfers between devices with their start and end apart: 28, of which 26 were waited for; matrix products, arithmetic and copies ran while one was open for 14% of the time, Pallas kernels for 0%

profile of v1, /device:TPU:0, one launch (start us, length us, event | category | flops | bytes accessed | tf_op | source)
XLA Modules:
  0.0 1021.7 jit_solution(699693094470632886)
XLA Ops:
  48.2 12.4 %collective-permute-done.1 = bf16[160,2048]{1,0:T(8,128)(2,1)} collective-permute-done((bf16[160,2048]{1,0:T(8,128)(2,1)S(1)}, bf16[160,2048]{1,0:T(8,128)(2,1)}, u32[]{:S(2)}, u32[]{:S(2)}) %collective-permute-start.1) | collective-permute-done | bytes 655392 | tf_op jit(solution)/shard_map/ppermute | solution.py:32
  61.7 10.9 %collective-permute-done.2 = bf16[160,2048]{1,0:T(8,128)(2,1)S(1)} collective-permute-done((bf16[160,2048]{1,0:T(8,128)(2,1)}, bf16[160,2048]{1,0:T(8,128)(2,1)S(1)}, u32[]{:S(2)}, u32[]{:S(2)}) %collective-permute-start.2) | collective-permute-done | bytes 655392 | tf_op jit(solution)/shard_map/ppermute | solution.py:27
  129.0 34.3 %all-to-all-done.1 = bf16[4,640,384]{1,2,0:T(8,128)(2,1)} async-done(((bf16[4,640,384]{1,2,0:T(8,128)(2,1)}), bf16[4,640,384]{1,2,0:T(8,128)(2,1)}, u32[]{:S(2)}, u32[]{:S(2)}) %all-to-all-start.1) | async-done | bytes 1966112 | tf_op jit(solution)/shard_map/all_to_all | solution.py:182
  190.2 10.9 %fusion.15 = bf16[2560,128]{1,0:T(8,128)(2,1)S(1)} fusion(bf16[2560,384]{1,0:T(8,128)(2,1)S(1)} %bitcast.242, f32[2560,2560]{0,1:T(8,128)} %copy-done.2, f32[2560]{0:T(1024)S(1)} %fusion.1, f32[2560]{0:T(1024)S(1)} %get-tuple-element.101), kind=kOutput, calls=%fused_computation.30 | convolution fusion | flops 1697710080 | bytes 27549696 | tf_op jit(solution)/shard_map/dot_general | solution.py:40
  201.1 12.7 %all_to_all.84 = bf16[4,640,128]{2,1,0:T(8,128)(2,1)S(1)} all-to-all(bf16[4,640,128]{2,1,0:T(8,128)(2,1)S(1)} %bitcast.249), channel_id=1, replica_groups=mesh['dp'=2,'row'=4,'col'=4] {'row'}, dimensions={0} | all-to-all | bytes 1310720 | tf_op jit(solution)/shard_map/all_to_all | solution.py:195
  227.2 43.1 %reduce-scatter.7.cloned.1.call-done = bf16[160,2048]{1,0:T(8,128)(2,1)} async-done(((bf16[640,2048]{1,0:T(8,128)(2,1)}), bf16[160,2048]{1,0:T(8,128)(2,1)}) %reduce-scatter.7.cloned.1.call-update) | async-done | bytes 655376 | tf_op jit(solution)/shard_map/reduce_scatter | solution.py:172
  276.2 15.6 %collective-permute-done.3 = bf16[160,2048]{1,0:T(8,128)(2,1)S(1)} collective-permute-done((bf16[160,2048]{1,0:T(8,128)(2,1)S(1)}, bf16[160,2048]{1,0:T(8,128)(2,1)S(1)}, u32[]{:S(2)}, u32[]{:S(2)}) %collective-permute-start.3) | collective-permute-done | bytes 655392 | tf_op jit(solution)/shard_map/ppermute | solution.py:27
  291.9 11.6 %collective-permute-start.5 = (bf16[160,2048]{1,0:T(8,128)(2,1)S(1)}, bf16[160,2048]{1,0:T(8,128)(2,1)S(1)}, u32[]{:S(2)}, u32[]{:S(2)}) collective-permute-start(bf16[160,2048]{1,0:T(8,128)(2,1)S(1)} %collective-permute-done.3), channel_id=1, source_target_pairs={{0,1},{1,2},{2,3},{3,0},{4,5},{5,6},{6,7},{7,4},{8,9},{9,10},{10,1... | collective-permute-start | bytes 1966088 | tf_op jit(solution)/shard_map/ppermute | solution.py:27
  304.0 14.6 %collective-permute-done.5 = bf16[160,2048]{1,0:T(8,128)(2,1)S(1)} collective-permute-done((bf16[160,2048]{1,0:T(8,128)(2,1)S(1)}, bf16[160,2048]{1,0:T(8,128)(2,1)S(1)}, u32[]{:S(2)}, u32[]{:S(2)}) %collective-permute-start.5) | collective-permute-done | bytes 655392 | tf_op jit(solution)/shard_map/ppermute | solution.py:27
  326.1 51.2 %all-gather.11.cloned.1.call-done = bf16[2048,2,2048]{2,1,0:T(2,128)(2,1)} async-done(((bf16[512,2,2048]{2,1,0:T(2,128)(2,1)}), bf16[2048,2,2048]{2,1,0:T(2,128)(2,1)}) %all-gather.11.cloned.1.call-update) | async-done | bytes 16777232 | tf_op jit(solution)/shard_map/all_gather | solution.py:159
  377.3 13.0 %copy.133 = bf16[256,8,2,2048]{3,1,2,0:T(8,128)(2,1)S(1)} copy(bf16[256,8,2,2048]{3,2,1,0:T(2,128)(2,1)} %bitcast.223) | data formatting | bytes 33554432
  390.3 11.3 %fusion.23 = f32[640,2048]{1,0:T(8,128)} fusion(f32[640,2048]{1,0:T(8,128)} %fusion.74, bf16[640,2048]{1,0:T(8,128)(2,1)S(1)} %copy-done.13, bf16[2048,4096]{1,0:T(8,128)(2,1)S(1)} %bitcast.219), kind=kOutput, calls=%fused_computation.35 | convolution fusion | flops 5370019840 | bytes 21495808 | tf_op jit(solution)/shard_map/dot_general | solution.py:40
  401.6 11.0 %multiply_convert_fusion.3 = (bf16[640,2048]{1,0:T(8,128)(2,1)}, f32[640,2048]{1,0:T(8,128)}) fusion(f32[640,2048]{1,0:T(8,128)} %fusion.23, f32[640,2048]{1,0:T(8,128)} %fusion.75, bf16[640,2048]{1,0:T(8,128)(2,1)S(1)} %copy-done.13, bf16[2048,4096]{1,0:T(8,128)(2,1)S(1)} %bitcast.220), kind=kOutput, calls=%fused_computation.23 | convolution fusion | flops 5377884160 | bytes 29360128 | tf_op jit(solution)/shard_map/dot_general | solution.py:40
  415.1 21.9 %all-gather.13.cloned.1.call-done = bf16[2048,2048]{1,0:T(8,128)(2,1)} async-done(((bf16[2048,512]{1,0:T(8,128)(2,1)}), bf16[2048,2048]{1,0:T(8,128)(2,1)}) %all-gather.13.cloned.1.call-update) | async-done | bytes 8388624 | tf_op jit(solution)/shard_map/all_gather | solution.py:160
  449.3 12.6 %all_to_all.85 = bf16[4,160,512]{2,1,0:T(8,128)(2,1)S(1)} all-to-all(bf16[4,160,512]{2,1,0:T(8,128)(2,1)S(1)} %bitcast.263), channel_id=1, replica_groups=mesh['dp'=2,'row'=4,'col'=4] {'row'}, dimensions={0} | all-to-all | bytes 1310720 | tf_op jit(solution)/shard_map/all_to_all | solution.py:163
  462.2 38.2 %reduce-scatter.9.cloned.1.call-done = bf16[160,2048]{1,0:T(8,128)(2,1)} async-done(((bf16[640,2048]{1,0:T(8,128)(2,1)}), bf16[160,2048]{1,0:T(8,128)(2,1)}) %reduce-scatter.9.cloned.1.call-update) | async-done | bytes 655376 | tf_op jit(solution)/shard_map/reduce_scatter | solution.py:172
  507.9 15.7 %collective-permute-done.6 = bf16[160,2048]{1,0:T(8,128)(2,1)S(1)} collective-permute-done((bf16[160,2048]{1,0:T(8,128)(2,1)S(1)}, bf16[160,2048]{1,0:T(8,128)(2,1)S(1)}, u32[]{:S(2)}, u32[]{:S(2)}) %collective-permute-start.6) | collective-permute-done | bytes 655392 | tf_op jit(solution)/shard_map/ppermute | solution.py:27
  523.5 11.2 %collective-permute-start.8 = (bf16[160,2048]{1,0:T(8,128)(2,1)S(1)}, bf16[160,2048]{1,0:T(8,128)(2,1)S(1)}, u32[]{:S(2)}, u32[]{:S(2)}) collective-permute-start(bf16[160,2048]{1,0:T(8,128)(2,1)S(1)} %collective-permute-done.6), channel_id=1, source_target_pairs={{0,1},{1,2},{2,3},{3,0},{4,5},{5,6},{6,7},{7,4},{8,9},{9,10},{10,1... | collective-permute-start | bytes 1966088 | tf_op jit(solution)/shard_map/ppermute | solution.py:27
  535.7 14.6 %collective-permute-done.8 = bf16[160,2048]{1,0:T(8,128)(2,1)S(1)} collective-permute-done((bf16[160,2048]{1,0:T(8,128)(2,1)S(1)}, bf16[160,2048]{1,0:T(8,128)(2,1)S(1)}, u32[]{:S(2)}, u32[]{:S(2)}) %collective-permute-start.8) | collective-permute-done | bytes 655392 | tf_op jit(solution)/shard_map/ppermute | solution.py:27
  556.1 15.9 %multiply_convert_fusion.1 = (bf16[640,2048]{1,0:T(8,128)(2,1)}, bf16[640,2048]{1,0:T(8,128)(2,1)}) fusion(f32[640,2048]{1,0:T(8,128)} %fusion.23, f32[640,2048]{1,0:T(8,128)} %get-tuple-element.104, f32[640,2048]{1,0:T(8,128)} %fusion.78, bf16[640,2048]{1,0:T(8,128)(2,1)S(1)} %constant_dynamic-update-slice_fusion.4, ...), kind=kOutput, calls=%fused_computation.20 | convolution fusion | flops 5387059200 | bytes 31981568 | tf_op jit(solution)/shard_map/dot_general | solution.py:44
  594.6 50.6 %reduce-scatter.11.cloned.1.call-done = bf16[160,2048]{1,0:T(8,128)(2,1)} async-done(((bf16[640,2048]{1,0:T(8,128)(2,1)}), bf16[160,2048]{1,0:T(8,128)(2,1)}) %reduce-scatter.11.cloned.1.call-update) | async-done | bytes 655376 | tf_op jit(solution)/shard_map/reduce_scatter | solution.py:172
  652.7 15.7 %collective-permute-done.9 = bf16[160,2048]{1,0:T(8,128)(2,1)S(1)} collective-permute-done((bf16[160,2048]{1,0:T(8,128)(2,1)S(1)}, bf16[160,2048]{1,0:T(8,128)(2,1)S(1)}, u32[]{:S(2)}, u32[]{:S(2)}) %collective-permute-start.9) | collective-permute-done | bytes 655392 | tf_op jit(solution)/shard_map/ppermute | solution.py:27
  668.3 11.5 %collective-permute-start.11 = (bf16[160,2048]{1,0:T(8,128)(2,1)S(1)}, bf16[160,2048]{1,0:T(8,128)(2,1)S(1)}, u32[]{:S(2)}, u32[]{:S(2)}) collective-permute-start(bf16[160,2048]{1,0:T(8,128)(2,1)S(1)} %collective-permute-done.9), channel_id=1, source_target_pairs={{0,1},{1,2},{2,3},{3,0},{4,5},{5,6},{6,7},{7,4},{8,9},{9,10},{10,1... | collective-permute-start | bytes 1966088 | tf_op jit(solution)/shard_map/ppermute | solution.py:27
  680.5 14.6 %collective-permute-done.11 = bf16[160,2048]{1,0:T(8,128)(2,1)S(1)} collective-permute-done((bf16[160,2048]{1,0:T(8,128)(2,1)S(1)}, bf16[160,2048]{1,0:T(8,128)(2,1)S(1)}, u32[]{:S(2)}, u32[]{:S(2)}) %collective-permute-start.11) | collective-permute-done | bytes 655392 | tf_op jit(solution)/shard_map/ppermute | solution.py:27
  700.8 12.9 %all_to_all.86 = bf16[4,640,128]{2,1,0:T(8,128)(2,1)S(1)} all-to-all(bf16[4,640,128]{2,1,0:T(8,128)(2,1)S(1)} %bitcast.251), channel_id=1, replica_groups=mesh['dp'=2,'row'=4,'col'=4] {'row'}, dimensions={0} | all-to-all | bytes 1310720 | tf_op jit(solution)/shard_map/all_to_all | solution.py:182
  713.8 20.4 %multiply_reduce_fusion = (f32[2560]{0:T(1024)S(1)}, f32[2560,2560]{0,1:T(8,128)}) fusion(f32[2560]{0:T(1024)S(1)} %copy-done.76, f32[2560,2560]{0,1:T(8,128)} %copy-done.2, f32[2560]{0:T(1024)S(1)} %copy-done.74, bf16[2560,128]{1,0:T(8,128)(2,1)S(1)} %bitcast.264, bf16[2560,384]{1,0:T(8,128)(2,1)S(1)} %bitcast.243), kind=kOutput, calls=%fused_computation.1 | convolution fusion | flops 1703933440 | bytes 53774336 | tf_op jit(solution)/shard_map/dot_general | solution.py:44
  734.2 22.4 %multiply_convert_fusion = bf16[2560,2560]{0,1:T(8,128)(2,1)} fusion(f32[2560,2560]{0,1:T(8,128)} %get-tuple-element.106, f32[2560]{0:T(1024)S(1)} %get-tuple-element.105, f32[2560]{0:T(1024)S(1)} %copy-done.76, f32[2560,2560]{0,1:T(8,128)} %copy-done.2, f32[2560]{0:T(1024)S(1)} %copy-done.74), kind=kLoop, calls=%fused_computation | loop fusion | flops 32768000 | bytes 65566720 | tf_op jit(solution)/shard_map/convert_element_type | solution.py:283
  772.4 11.1 %fusion.20 = bf16[2560,128]{0,1:T(8,128)(2,1)S(1)} fusion(bf16[2560,128]{1,0:T(8,128)(2,1)S(1)} %bitcast.265, f32[2560,2560]{0,1:T(8,128)} %copy-done.2, f32[2560]{0:T(1024)S(1)} %copy-done.76, f32[2560]{0:T(1024)S(1)} %copy-done.74), kind=kOutput, calls=%fused_computation.33 | convolution fusion | flops 1697710080 | bytes 27545600 | tf_op jit(solution)/shard_map/dot_general | solution.py:48
  799.6 17.6 %all-to-all-done.6 = bf16[4,640,384]{2,1,0:T(8,128)(2,1)S(1)} async-done(((bf16[4,640,384]{2,1,0:T(8,128)(2,1)}), bf16[4,640,384]{2,1,0:T(8,128)(2,1)S(1)}, u32[]{:S(2)}, u32[]{:S(2)}) %all-to-all-start.6) | async-done | bytes 1966112 | tf_op jit(solution)/shard_map/all_to_all | solution.py:195
  893.0 12.4 %all-reduce.7.cloned.1.call-done = bf16[16,8192]{1,0:T(8,128)(2,1)} async-done(((bf16[16,8192]{1,0:T(8,128)(2,1)}), bf16[16,8192]{1,0:T(8,128)(2,1)}) %all-reduce.7.cloned.1.call-update) | async-done | bytes 262160
  906.4 36.0 %all-reduce.5.cloned.1.call-done = bf16[4,7,4,512]{3,2,0,1:T(4,128)(2,1)} async-done(((bf16[4,7,4,512]{3,2,0,1:T(4,128)(2,1)}), bf16[4,7,4,512]{3,2,0,1:T(4,128)(2,1)}) %all-reduce.5.cloned.1.call-update) | async-done | bytes 114704
  956.7 40.1 %reduce-scatter.13.cloned.1.call-done = bf16[160,2048]{1,0:T(8,128)(2,1)} async-done(((bf16[640,2048]{1,0:T(8,128)(2,1)}), bf16[160,2048]{1,0:T(8,128)(2,1)}) %reduce-scatter.13.cloned.1.call-update) | async-done | bytes 655376 | tf_op jit(solution)/shard_map/reduce_scatter | solution.py:172
  (393 shorter events, 356.8 us)
Async XLA Ops:
  7.2 296.3 %copy-start = (f32[2,8,16,2048]{3,2,1,0:T(8,128)S(1)}, f32[2,8,16,2048]{3,2,1,0:T(8,128)}, u32[]{:S(2)}) copy-start(f32[2,8,16,2048]{3,2,1,0:T(8,128)} %param.41) | copy-start | bytes 6291460
  7.2 69.9 %all-gather.7.cloned.1.call-start = ((), (), s32[]{:S(2)}) async-start(), calls=%async_computation.13 | async-start | bytes 7864320 | tf_op jit(solution)/shard_map/all_gather | solution.py:155
  10.0 15.7 %all-to-all-start = ((bf16[4,160,512]{2,1,0:T(8,128)(2,1)}), bf16[4,160,512]{2,1,0:T(8,128)(2,1)S(1)}, u32[]{:S(2)}, u32[]{:S(2)}) async-start(bf16[4,160,512]{2,1,0:T(8,128)(2,1)} %bitcast), calls=%async_computation | async-start | bytes 1310720 | tf_op jit(solution)/shard_map/all_to_all | solution.py:163
  25.8 20.9 %collective-permute-start = (bf16[160,2048]{1,0:T(8,128)(2,1)S(1)}, bf16[160,2048]{1,0:T(8,128)(2,1)}, u32[]{:S(2)}, u32[]{:S(2)}) collective-permute-start(bf16[160,2048]{1,0:T(8,128)(2,1)S(1)} %bitcast.231), channel_id=1, source_target_pairs={{0,1},{1,2},{2,3},{3,0},{4,5},{5,6},{6,7},{7,4},{8,9},{9,10},{10,1... | collective-permute-start | bytes 1966088 | tf_op jit(solution)/shard_map/ppermute | solution.py:27
  31.1 29.5 %collective-permute-start.1 = (bf16[160,2048]{1,0:T(8,128)(2,1)S(1)}, bf16[160,2048]{1,0:T(8,128)(2,1)}, u32[]{:S(2)}, u32[]{:S(2)}) collective-permute-start(bf16[160,2048]{1,0:T(8,128)(2,1)S(1)} %bitcast.232), channel_id=1, source_target_pairs={{0,3},{1,0},{2,1},{3,2},{4,7},{5,4},{6,5},{7,6},{8,11},{9,8},{10,9... | collective-permute-start | bytes 1966088 | tf_op jit(solution)/shard_map/ppermute | solution.py:32
  46.6 26.0 %collective-permute-start.2 = (bf16[160,2048]{1,0:T(8,128)(2,1)}, bf16[160,2048]{1,0:T(8,128)(2,1)S(1)}, u32[]{:S(2)}, u32[]{:S(2)}) collective-permute-start(bf16[160,2048]{1,0:T(8,128)(2,1)} %collective-permute-done), channel_id=1, source_target_pairs={{0,1},{1,2},{2,3},{3,0},{4,5},{5,6},{6,7},{7,4},{8,9},{9,10},{10,1... | collective-permute-start | bytes 1966088 | tf_op jit(solution)/shard_map/ppermute | solution.py:27
  123.2 40.2 %all-to-all-start.1 = ((bf16[4,640,384]{1,2,0:T(8,128)(2,1)}), bf16[4,640,384]{1,2,0:T(8,128)(2,1)}, u32[]{:S(2)}, u32[]{:S(2)}) async-start(bf16[4,640,384]{1,2,0:T(8,128)(2,1)} %bitcast.236), calls=%async_computation.1 | async-start | bytes 3932160 | tf_op jit(solution)/shard_map/all_to_all | solution.py:182
  127.7 87.3 %all-gather.9.cloned.1.call-start = ((), (), s32[]{:S(2)}) async-start(), calls=%async_computation.14 | async-start | bytes 2621440 | tf_op jit(solution)/shard_map/all_gather | solution.py:158
  128.5 141.8 %reduce-scatter.7.cloned.1.call-start = ((), (), s32[]{:S(2)}) async-start(), calls=%async_computation.15 | async-start | bytes 3276800 | tf_op jit(solution)/shard_map/reduce_scatter | solution.py:172
  220.7 156.6 %all-gather.11.cloned.1.call-start = ((), (), s32[]{:S(2)}) async-start(), calls=%async_computation.16 | async-start | bytes 20971520 | tf_op jit(solution)/shard_map/all_gather | solution.py:159
  221.3 215.7 %all-gather.13.cloned.1.call-start = ((), (), s32[]{:S(2)}) async-start(), calls=%async_computation.17 | async-start | bytes 10485760 | tf_op jit(solution)/shard_map/all_gather | solution.py:160
  221.9 278.6 %reduce-scatter.9.cloned.1.call-start = ((), (), s32[]{:S(2)}) async-start(), calls=%async_computation.18 | async-start | bytes 3276800 | tf_op jit(solution)/shard_map/reduce_scatter | solution.py:172
  272.4 19.5 %collective-permute-start.3 = (bf16[160,2048]{1,0:T(8,128)(2,1)S(1)}, bf16[160,2048]{1,0:T(8,128)(2,1)S(1)}, u32[]{:S(2)}, u32[]{:S(2)}) collective-permute-start(bf16[160,2048]{1,0:T(8,128)(2,1)S(1)} %get-tuple-element.63), channel_id=1, source_target_pairs={{0,1},{1,2},{2,3},{3,0},{4,5},{5,6},{6,7},{7,4},{8,9},{9,10},{10,1... | collective-permute-start | bytes 1966088 | tf_op jit(solution)/shard_map/ppermute | solution.py:27
  273.1 30.9 %collective-permute-start.4 = (bf16[160,2048]{1,0:T(8,128)(2,1)S(1)}, bf16[160,2048]{1,0:T(8,128)(2,1)S(1)}, u32[]{:S(2)}, u32[]{:S(2)}) collective-permute-start(bf16[160,2048]{1,0:T(8,128)(2,1)S(1)} %get-tuple-element.63), channel_id=1, source_target_pairs={{0,3},{1,0},{2,1},{3,2},{4,7},{5,4},{6,5},{7,6},{8,11},{9,8},{10,9... | collective-permute-start | bytes 1966088 | tf_op jit(solution)/shard_map/ppermute | solution.py:32
  291.9 26.7 %collective-permute-start.5 = (bf16[160,2048]{1,0:T(8,128)(2,1)S(1)}, bf16[160,2048]{1,0:T(8,128)(2,1)S(1)}, u32[]{:S(2)}, u32[]{:S(2)}) collective-permute-start(bf16[160,2048]{1,0:T(8,128)(2,1)S(1)} %collective-permute-done.3), channel_id=1, source_target_pairs={{0,1},{1,2},{2,3},{3,0},{4,5},{5,6},{6,7},{7,4},{8,9},{9,10},{10,1... | collective-permute-start | bytes 1966088 | tf_op jit(solution)/shard_map/ppermute | solution.py:27
  448.2 197.0 %reduce-scatter.11.cloned.1.call-start = ((), (), s32[]{:S(2)}) async-start(), calls=%async_computation.19 | async-start | bytes 3276800 | tf_op jit(solution)/shard_map/reduce_scatter | solution.py:172
  462.2 186.1 %copy-start.3 = (f32[4,20,8,512]{3,2,0,1:T(8,128)}, f32[4,20,8,512]{3,2,0,1:T(8,128)S(1)}, u32[]{:S(2)}) copy-start(f32[4,20,8,512]{3,2,0,1:T(8,128)S(1)} %copy.130) | copy-start | bytes 3932164
  504.0 19.5 %collective-permute-start.6 = (bf16[160,2048]{1,0:T(8,128)(2,1)S(1)}, bf16[160,2048]{1,0:T(8,128)(2,1)S(1)}, u32[]{:S(2)}, u32[]{:S(2)}) collective-permute-start(bf16[160,2048]{1,0:T(8,128)(2,1)S(1)} %get-tuple-element.61), channel_id=1, source_target_pairs={{0,1},{1,2},{2,3},{3,0},{4,5},{5,6},{6,7},{7,4},{8,9},{9,10},{10,1... | collective-permute-start | bytes 1966088 | tf_op jit(solution)/shard_map/ppermute | solution.py:27
  504.7 30.9 %collective-permute-start.7 = (bf16[160,2048]{1,0:T(8,128)(2,1)S(1)}, bf16[160,2048]{1,0:T(8,128)(2,1)S(1)}, u32[]{:S(2)}, u32[]{:S(2)}) collective-permute-start(bf16[160,2048]{1,0:T(8,128)(2,1)S(1)} %get-tuple-element.61), channel_id=1, source_target_pairs={{0,3},{1,0},{2,1},{3,2},{4,7},{5,4},{6,5},{7,6},{8,11},{9,8},{10,9... | collective-permute-start | bytes 1966088 | tf_op jit(solution)/shard_map/ppermute | solution.py:32
  523.5 26.7 %collective-permute-start.8 = (bf16[160,2048]{1,0:T(8,128)(2,1)S(1)}, bf16[160,2048]{1,0:T(8,128)(2,1)S(1)}, u32[]{:S(2)}, u32[]{:S(2)}) collective-permute-start(bf16[160,2048]{1,0:T(8,128)(2,1)S(1)} %collective-permute-done.6), channel_id=1, source_target_pairs={{0,1},{1,2},{2,3},{3,0},{4,5},{5,6},{6,7},{7,4},{8,9},{9,10},{10,1... | collective-permute-start | bytes 1966088 | tf_op jit(solution)/shard_map/ppermute | solution.py:27
  594.6 50.7 %copy-start.25 = (bf16[160,2048]{1,0:T(8,128)(2,1)S(1)}, bf16[160,2048]{1,0:T(8,128)(2,1)}, u32[]{:S(2)}) copy-start(bf16[160,2048]{1,0:T(8,128)(2,1)} %reduce-scatter.9.cloned.1.call-done) | copy-start | bytes 1966084
  594.6 50.7 %copy-start.27 = (bf16[160,2048]{1,0:T(8,128)(2,1)S(1)}, bf16[160,2048]{1,0:T(8,128)(2,1)}, u32[]{:S(2)}) copy-start(bf16[160,2048]{1,0:T(8,128)(2,1)} %reduce-scatter.7.cloned.1.call-done) | copy-start | bytes 1966084
  648.8 19.5 %collective-permute-start.9 = (bf16[160,2048]{1,0:T(8,128)(2,1)S(1)}, bf16[160,2048]{1,0:T(8,128)(2,1)S(1)}, u32[]{:S(2)}, u32[]{:S(2)}) collective-permute-start(bf16[160,2048]{1,0:T(8,128)(2,1)S(1)} %get-tuple-element.59), channel_id=1, source_target_pairs={{0,1},{1,2},{2,3},{3,0},{4,5},{5,6},{6,7},{7,4},{8,9},{9,10},{10,1... | collective-permute-start | bytes 1966088 | tf_op jit(solution)/shard_map/ppermute | solution.py:27
  649.5 30.9 %collective-permute-start.10 = (bf16[160,2048]{1,0:T(8,128)(2,1)S(1)}, bf16[160,2048]{1,0:T(8,128)(2,1)S(1)}, u32[]{:S(2)}, u32[]{:S(2)}) collective-permute-start(bf16[160,2048]{1,0:T(8,128)(2,1)S(1)} %get-tuple-element.59), channel_id=1, source_target_pairs={{0,3},{1,0},{2,1},{3,2},{4,7},{5,4},{6,5},{7,6},{8,11},{9,8},{10,9... | collective-permute-start | bytes 1966088 | tf_op jit(solution)/shard_map/ppermute | solution.py:32
  668.3 26.8 %collective-permute-start.11 = (bf16[160,2048]{1,0:T(8,128)(2,1)S(1)}, bf16[160,2048]{1,0:T(8,128)(2,1)S(1)}, u32[]{:S(2)}, u32[]{:S(2)}) collective-permute-start(bf16[160,2048]{1,0:T(8,128)(2,1)S(1)} %collective-permute-done.9), channel_id=1, source_target_pairs={{0,1},{1,2},{2,3},{3,0},{4,5},{5,6},{6,7},{7,4},{8,9},{9,10},{10,1... | collective-permute-start | bytes 1966088 | tf_op jit(solution)/shard_map/ppermute | solution.py:27
  789.2 28.0 %all-to-all-start.6 = ((bf16[4,640,384]{2,1,0:T(8,128)(2,1)}), bf16[4,640,384]{2,1,0:T(8,128)(2,1)S(1)}, u32[]{:S(2)}, u32[]{:S(2)}) async-start(bf16[4,640,384]{2,1,0:T(8,128)(2,1)} %bitcast.237), calls=%async_computation.9 | async-start | bytes 3932160 | tf_op jit(solution)/shard_map/all_to_all | solution.py:195
  792.9 77.3 %reduce-scatter.15.cloned.1.call-start = ((), (), s32[]{:S(2)}) async-start(), calls=%async_computation.21 | async-start | bytes 573440 | tf_op jit(solution)/shard_map/reduce_scatter | solution.py:305
  851.0 54.4 %all-reduce.7.cloned.1.call-start = ((), (), s32[]{:S(2)}) async-start(), calls=%async_computation.23 | async-start | bytes 524288
  859.8 82.5 %all-reduce.5.cloned.1.call-start = ((), (), s32[]{:S(2)}) async-start(), calls=%async_computation.22 | async-start | bytes 229376
  871.8 125.0 %reduce-scatter.13.cloned.1.call-start = ((), (), s32[]{:S(2)}) async-start(), calls=%async_computation.20 | async-start | bytes 3276800 | tf_op jit(solution)/shard_map/reduce_scatter | solution.py:172
  878.7 14.3 %all-to-all-start.3 = ((bf16[160,4,512]{2,0,1:T(8,128)(2,1)}), bf16[160,4,512]{2,0,1:T(8,128)(2,1)S(1)}, u32[]{:S(2)}, u32[]{:S(2)}) async-start(bf16[160,4,512]{2,0,1:T(8,128)(2,1)} %bitcast.209), calls=%async_computation.5 | async-start | bytes 1310720 | tf_op jit(solution)/shard_map/all_to_all | solution.py:166
  999.1 13.8 %all-to-all-start.7 = ((bf16[160,4,512]{2,0,1:T(8,128)(2,1)}), bf16[160,4,512]{2,0,1:T(8,128)(2,1)S(1)}, u32[]{:S(2)}, u32[]{:S(2)}) async-start(bf16[160,4,512]{2,0,1:T(8,128)(2,1)} %bitcast.208), calls=%async_computation.11 | async-start | bytes 1310720 | tf_op jit(solution)/shard_map/all_to_all | solution.py:166
  (84 other events, 802.0 us)
Sparse Core Ops, SparseCore 0:
  10.1 52.1 all-gather.6
  130.1 32.6 all-gather.8
  220.8 49.3 reduce-scatter.6
  271.7 105.5 all-gather.10
  378.7 58.2 all-gather.12
  448.3 52.0 reduce-scatter.8
  594.7 50.4 reduce-scatter.10
  851.1 19.0 reduce-scatter.14
  873.2 32.1 all-reduce.6
  908.3 34.0 all-reduce.4
  944.7 52.0 reduce-scatter.12
